TPU v7x, 32 devices: a whole 2x2x4 slice. The times are simulated.
32 devices in a mesh: expert: 2 (over y), hidden: 4 (over z), dp: 4 (over x, core).
Axes of the slice: x: 2, y: 2, z: 4, core: 2. Of those that a mesh axis runs over, the one named last changes fastest.
Arguments:
- tokens: bfloat16 [2, 4, 512, 2048], P('expert', 'dp', None, 'hidden'), may hold values from -6 to 6
- grad_out: bfloat16 [2, 4, 512, 2048], P('expert', 'dp', None, 'hidden'), may hold values from -0.25 to 0.25
- gate_weight: bfloat16 [4, 2048, 512], P('expert', 'dp', 'hidden'), may hold values from -0.125 to 0.125
- up_weight: bfloat16 [4, 2048, 512], P('expert', 'dp', 'hidden'), may hold values from -0.125 to 0.125
- down_weight: bfloat16 [4, 512, 2048], P('expert', 'hidden', 'dp'), may hold values from -0.25 to 0.25
- matching: int32 [2], replicated, may hold values from 0 to 1, each once
- block_counts: int32 [2, 4, 2], P('expert', 'dp'), may hold values from 0 to 4, as said below
Outputs:
- grad_gate: bfloat16 [4, 2048, 512], P('expert', 'dp', 'hidden')
- grad_up: bfloat16 [4, 2048, 512], P('expert', 'dp', 'hidden')
- grad_down: bfloat16 [4, 512, 2048], P('expert', 'hidden', 'dp')
Inputs may be any that keep to these rules, and one draw needn't show every extreme that they name: `matching`: each expert index appears once. `block_counts`: the 2 counts of one expert index and data index sum to at most 4; on some device one count equals 4.
All inputs are finite; a program needn't handle non-finite values.
Results may differ from a plain program's by a relative error of at most 0.008.
Values may be sent and summed in bfloat16 or wider, within the bound.
A program may use at most 64 MiB of HBM per device.

v0:
```python
import jax
import jax.numpy as jnp
from jax import lax
from jax.sharding import PartitionSpec as P

BLOCK = 128


def contract_rows(left, right):
    return lax.dot_general(
        left, right, (((0,), (0,)), ((), ())), preferred_element_type=jnp.float32
    )


def block_owners(counts, blocks):
    bounds = jnp.cumsum(counts)
    index = jnp.arange(blocks, dtype=jnp.int32)
    owner = jnp.sum((index[:, None] >= bounds[None, :]).astype(jnp.int32), axis=1)
    owner = jnp.minimum(owner, counts.shape[0] - 1)
    alive = (index < bounds[-1]).astype(jnp.float32)
    return (owner, alive)


def add_into(total, term, expert):
    current = lax.dynamic_index_in_dim(total, expert, 0, keepdims=True)
    return lax.dynamic_update_index_in_dim(total, current + term[None], expert, 0)


def expert_terms(row_blocks, grad_blocks, weight_gate, weight_up, weight_down, owner, alive):
    zeros_gate = jnp.zeros(weight_gate.shape, jnp.float32)
    zeros_down = jnp.zeros(weight_down.shape, jnp.float32)

    def step(carry, inputs):
        total_gate, total_up, total_down = carry
        row_block, grad_block, expert, live = inputs
        gate_matrix = lax.dynamic_index_in_dim(weight_gate, expert, 0, keepdims=False)
        up_matrix = lax.dynamic_index_in_dim(weight_up, expert, 0, keepdims=False)
        down_matrix = lax.dynamic_index_in_dim(weight_down, expert, 0, keepdims=False)
        gate_value = jnp.dot(row_block, gate_matrix, preferred_element_type=jnp.float32)
        up_value = jnp.dot(row_block, up_matrix, preferred_element_type=jnp.float32)
        sigmoid_gate = jax.nn.sigmoid(gate_value)
        activated = gate_value * sigmoid_gate
        hidden = (activated * up_value * live).astype(jnp.bfloat16)
        grad_hidden = lax.dot_general(
            grad_block, down_matrix, (((1,), (1,)), ((), ())), preferred_element_type=jnp.float32
        )
        grad_gate = (
            grad_hidden * up_value * sigmoid_gate * (1.0 + gate_value * (1.0 - sigmoid_gate)) * live
        ).astype(jnp.bfloat16)
        grad_up = (grad_hidden * activated * live).astype(jnp.bfloat16)
        total_gate = add_into(total_gate, contract_rows(row_block, grad_gate), expert)
        total_up = add_into(total_up, contract_rows(row_block, grad_up), expert)
        total_down = add_into(total_down, contract_rows(hidden, grad_block), expert)
        return ((total_gate, total_up, total_down), None)

    totals, unused = lax.scan(
        step, (zeros_gate, zeros_gate, zeros_down), (row_blocks, grad_blocks, owner, alive)
    )
    return totals


def relocate(arrays, matching):
    groups = lax.axis_size("expert")
    joined = jnp.concatenate([array_piece.reshape(groups, -1) for array_piece in arrays], axis=1)
    spread = lax.all_to_all(joined, "expert", split_axis=0, concat_axis=0, tiled=True)
    ordered = jnp.take(spread, matching, axis=0)
    settled = lax.all_to_all(ordered, "expert", split_axis=0, concat_axis=0, tiled=True)
    pieces = []
    offset = 0
    for array_piece in arrays:
        length = array_piece.size // groups
        pieces.append(settled[:, offset : offset + length].reshape(array_piece.shape))
        offset = offset + length
    return pieces


def on_device(tokens, grad_out, gate_weight, up_weight, down_weight, matching, block_counts):
    moved = relocate((gate_weight, up_weight, down_weight), matching)
    weight_gate, weight_up, weight_down = (
        lax.all_gather(moved[0], "dp", axis=1, tiled=True),
        lax.all_gather(moved[1], "dp", axis=1, tiled=True),
        lax.all_gather(moved[2], "dp", axis=2, tiled=True),
    )
    rows_full, grads_full = (
        lax.all_gather(tokens[0, 0], "hidden", axis=1, tiled=True),
        lax.all_gather(grad_out[0, 0], "hidden", axis=1, tiled=True),
    )
    blocks = rows_full.shape[0] // BLOCK
    width = rows_full.shape[1]
    owner, alive = block_owners(block_counts[0, 0], blocks)
    totals = expert_terms(
        rows_full.reshape(blocks, BLOCK, width),
        grads_full.reshape(blocks, BLOCK, width),
        weight_gate,
        weight_up,
        weight_down,
        owner,
        alive,
    )
    summed = (
        lax.psum_scatter(
            totals[0].astype(jnp.bfloat16), "dp", scatter_dimension=1, tiled=True
        ).astype(jnp.float32),
        lax.psum_scatter(
            totals[1].astype(jnp.bfloat16), "dp", scatter_dimension=1, tiled=True
        ).astype(jnp.float32),
        lax.psum_scatter(
            totals[2].astype(jnp.bfloat16), "dp", scatter_dimension=2, tiled=True
        ).astype(jnp.float32),
    )
    return (
        summed[0].astype(jnp.bfloat16),
        summed[1].astype(jnp.bfloat16),
        summed[2].astype(jnp.bfloat16),
    )


def solution(mesh):
    in_specs = (
        P("expert", "dp", None, "hidden"),
        P("expert", "dp", None, "hidden"),
        P("expert", "dp", "hidden"),
        P("expert", "dp", "hidden"),
        P("expert", "hidden", "dp"),
        P(),
        P("expert", "dp", None),
    )
    out_specs = (
        P("expert", "dp", "hidden"),
        P("expert", "dp", "hidden"),
        P("expert", "hidden", "dp"),
    )
    return jax.shard_map(
        on_device, mesh=mesh, in_specs=in_specs, out_specs=out_specs, check_vma=False
    )
```

profile of v0, /device:TPU:0, one launch (start us, length us, event | category | flops | bytes accessed | tf_op | source)
XLA Modules:
  0.0 368.9 jit_solution(15848804387790991597)
XLA Ops:
  10.0 9.9 %maximum_bitcast_fusion = bf16[2,1,196608]{2,0,1:T(2,128)(2,1)S(1)} fusion(bf16[2,65536]{1,0:T(2,128)(2,1)S(1)} %bitcast.118, bf16[2,65536]{1,0:T(2,128)(2,1)S(1)} %get-tuple-element.92, bf16[2,65536]{1,0:T(2,128)(2,1)S(1)} %get-tuple-element.93), kind=kLoop, calls=%fused_computation.51 | loop fusion | flops 2359296 | bytes 1572864 | tf_op jit(solution)/shard_map/all_to_all | solution.py:65
  20.4 2.6 reduce
  24.5 4.3 %all-to-all-start = ((bf16[2,2,98304]{2,1,0:T(2,128)(2,1)}), bf16[2,2,98304]{2,1,0:T(2,128)(2,1)S(1)}, u32[]{:S(2)}, u32[]{:S(2)}) async-start(bf16[2,2,98304]{2,1,0:T(2,128)(2,1)} %reshape.103), calls=%async_computation | async-start | bytes 1572864 | tf_op jit(solution)/shard_map/all_to_all | solution.py:65
  28.8 11.5 %all-to-all-done = bf16[2,2,98304]{2,1,0:T(2,128)(2,1)S(1)} async-done(((bf16[2,2,98304]{2,1,0:T(2,128)(2,1)}), bf16[2,2,98304]{2,1,0:T(2,128)(2,1)S(1)}, u32[]{:S(2)}, u32[]{:S(2)}) %all-to-all-start) | async-done | bytes 786464 | tf_op jit(solution)/shard_map/all_to_all | solution.py:65
  41.0 2.5 copy.31
  46.2 7.0 %broadcast_select_fusion = bf16[2,1,196608]{2,0,1:T(2,128)(2,1)S(1)} fusion(pred[2]{0:T(512)(128)(4,1)S(1)} %compare_and_fusion, bf16[2,98304]{1,0:T(2,128)(2,1)S(1)} %gather_fusion.1, bf16[2,98304]{1,0:T(2,128)(2,1)S(1)} %gather_fusion), kind=kLoop, calls=%fused_computation.50 | loop fusion | flops 1966080 | bytes 1572866 | tf_op jit(solution)/shard_map/jit(_take)/select_n | solution.py:66
  53.2 2.6 reduce.1
  56.4 12.9 %all_to_all.21 = bf16[2,2,98304]{2,1,0:T(2,128)(2,1)S(1)} all-to-all(bf16[2,2,98304]{2,1,0:T(2,128)(2,1)S(1)} %reshape.105), channel_id=1, replica_groups=mesh['expert'=2,'hidden'=4,'dp'=4] {'expert'}, dimensions={0} | all-to-all | bytes 1572864 | tf_op jit(solution)/shard_map/all_to_all | solution.py:67
  70.0 2.5 copy.30
  78.3 12.6 %all-gather.12.cloned.1.call-done = bf16[2,2048,128]{2,1,0:T(8,128)(2,1)} async-done(((bf16[2,512,128]{2,1,0:T(8,128)(2,1)}), bf16[2,2048,128]{2,1,0:T(8,128)(2,1)}) %all-gather.12.cloned.1.call-update) | async-done | bytes 1048592 | tf_op jit(solution)/shard_map/all_gather | solution.py:80
  90.9 18.9 %all-gather.10.cloned.1.call-done = bf16[2,2048,128]{2,1,0:T(8,128)(2,1)} async-done(((bf16[2,512,128]{2,1,0:T(8,128)(2,1)}), bf16[2,2048,128]{2,1,0:T(8,128)(2,1)}) %all-gather.10.cloned.1.call-update) | async-done | bytes 1048592 | tf_op jit(solution)/shard_map/all_gather | solution.py:81
  109.8 18.9 %all-gather.8.cloned.1.call-done = bf16[2,128,2048]{2,1,0:T(8,128)(2,1)} async-done(((bf16[2,128,512]{2,1,0:T(8,128)(2,1)}), bf16[2,128,2048]{2,1,0:T(8,128)(2,1)}) %all-gather.8.cloned.1.call-update) | async-done | bytes 1048592 | tf_op jit(solution)/shard_map/all_gather | solution.py:82
  128.7 47.1 %all-gather.14.cloned.1.call-done = bf16[1,1,512,2048]{3,2,1,0:T(8,128)(2,1)} async-done(((bf16[1,1,512,512]{3,2,1,0:T(8,128)(2,1)}), bf16[1,1,512,2048]{3,2,1,0:T(8,128)(2,1)}) %all-gather.14.cloned.1.call-update) | async-done | bytes 2097168 | tf_op jit(solution)/shard_map/all_gather | solution.py:85
  175.8 45.9 %all-gather.16.cloned.1.call-done = bf16[1,1,512,2048]{3,2,1,0:T(8,128)(2,1)} async-done(((bf16[1,1,512,512]{3,2,1,0:T(8,128)(2,1)}), bf16[1,1,512,2048]{3,2,1,0:T(8,128)(2,1)}) %all-gather.16.cloned.1.call-update) | async-done | bytes 2097168 | tf_op jit(solution)/shard_map/all_gather | solution.py:86
  226.2 53.4 %while.14 = (s32[]{:T(128)}, f32[2,2048,128]{2,1,0:T(8,128)}, f32[2,2048,128]{2,1,0:T(8,128)}, f32[2,128,2048]{2,1,0:T(8,128)}, s32[4]{0:T(128)S(1)}, /*index=5*...) while((s32[]{:T(128)}, f32[2,2048,128]{2,1,0:T(8,128)}, ...), condition=%wide.region_3.4_spmd, body=%wide.region_2.3_spmd.sunk | while | flops 403849216 | bytes 61997988 | solution.py:56
  236.1 2.1 fusion.74
  249.4 2.1 fusion.74
  262.8 2.1 fusion.74
  276.1 2.1 fusion.74
  279.6 2.7 convert_element_type.34
  282.4 2.9 convert_element_type.32
  286.5 19.6 %reduce-scatter.8.cloned.1.call-done = bf16[2,128,512]{2,1,0:T(8,128)(2,1)} async-done(((bf16[2,128,2048]{2,1,0:T(8,128)(2,1)}), bf16[2,128,512]{2,1,0:T(8,128)(2,1)}) %reduce-scatter.8.cloned.1.call-update) | async-done | bytes 262160 | tf_op jit(solution)/shard_map/reduce_scatter | solution.py:107
  306.1 27.9 %reduce-scatter.4.cloned.1.call-done = bf16[2,512,128]{2,1,0:T(8,128)(2,1)} async-done(((bf16[2,2048,128]{2,1,0:T(8,128)(2,1)}), bf16[2,512,128]{2,1,0:T(8,128)(2,1)}) %reduce-scatter.4.cloned.1.call-update) | async-done | bytes 262160 | tf_op jit(solution)/shard_map/reduce_scatter | solution.py:101
  334.1 27.9 %reduce-scatter.6.cloned.1.call-done = bf16[2,512,128]{2,1,0:T(8,128)(2,1)} async-done(((bf16[2,2048,128]{2,1,0:T(8,128)(2,1)}), bf16[2,512,128]{2,1,0:T(8,128)(2,1)}) %reduce-scatter.6.cloned.1.call-update) | async-done | bytes 262160 | tf_op jit(solution)/shard_map/reduce_scatter | solution.py:104
  (128 shorter events, 57.7 us)
Async XLA Ops:
  20.4 8.4 %copy-start.9 = (s32[2]{0:T(128)S(1)}, s32[2]{0:T(128)}, u32[]{:S(2)}) copy-start(s32[2]{0:T(128)} %param.14) | copy-start | bytes 28
  24.5 15.8 %all-to-all-start = ((bf16[2,2,98304]{2,1,0:T(2,128)(2,1)}), bf16[2,2,98304]{2,1,0:T(2,128)(2,1)S(1)}, u32[]{:S(2)}, u32[]{:S(2)}) async-start(bf16[2,2,98304]{2,1,0:T(2,128)(2,1)} %reshape.103), calls=%async_computation | async-start | bytes 1572864 | tf_op jit(solution)/shard_map/all_to_all | solution.py:65
  28.8 62.2 %all-gather.12.cloned.1.call-start = ((), (), s32[]{:S(2)}) async-start(), calls=%async_computation.7 | async-start | bytes 1310720 | tf_op jit(solution)/shard_map/all_gather | solution.py:80
  73.1 3.8 %copy-start.10 = (s32[1,1,2]{2,1,0:T(1,128)S(1)}, s32[1,1,2]{2,1,0:T(1,128)}, u32[]{:S(2)}) copy-start(s32[1,1,2]{2,1,0:T(1,128)} %param.15) | copy-start | bytes 28
  73.8 36.0 %all-gather.10.cloned.1.call-start = ((), (), s32[]{:S(2)}) async-start(), calls=%async_computation.6 | async-start | bytes 1310720 | tf_op jit(solution)/shard_map/all_gather | solution.py:81
  74.6 54.0 %all-gather.8.cloned.1.call-start = ((), (), s32[]{:S(2)}) async-start(), calls=%async_computation.5 | async-start | bytes 1310720 | tf_op jit(solution)/shard_map/all_gather | solution.py:82
  75.4 100.3 %all-gather.14.cloned.1.call-start = ((), (), s32[]{:S(2)}) async-start(), calls=%async_computation.11 | async-start | bytes 2621440 | tf_op jit(solution)/shard_map/all_gather | solution.py:85
  76.0 145.7 %all-gather.16.cloned.1.call-start = ((), (), s32[]{:S(2)}) async-start(), calls=%async_computation.12 | async-start | bytes 2621440 | tf_op jit(solution)/shard_map/all_gather | solution.py:86
  76.6 229.5 %reduce-scatter.8.cloned.1.call-start = ((), (), s32[]{:S(2)}) async-start(), calls=%async_computation.10 | async-start | bytes 1310720 | tf_op jit(solution)/shard_map/reduce_scatter | solution.py:107
  223.2 3.1 copy-start
  223.2 3.1 copy-start.8
  228.8 3.9 %copy-start.1 = (f32[2,2048,128]{2,1,0:T(8,128)S(1)}, f32[2,2048,128]{2,1,0:T(8,128)}, u32[]{:S(2)}) copy-start(f32[2,2048,128]{2,1,0:T(8,128)} %get-tuple-element.177) | copy-start | bytes 6291460 | tf_op jit(solution)/shard_map/while
  233.7 4.5 %copy-start.2 = (f32[2,2048,128]{2,1,0:T(8,128)}, f32[2,2048,128]{2,1,0:T(8,128)S(1)}, u32[]{:S(2)}) copy-start(f32[2,2048,128]{2,1,0:T(8,128)S(1)} %fusion.73) | copy-start | bytes 6291460 | tf_op jit(solution)/shard_map/while
  242.1 3.9 %copy-start.1 = (f32[2,2048,128]{2,1,0:T(8,128)S(1)}, f32[2,2048,128]{2,1,0:T(8,128)}, u32[]{:S(2)}) copy-start(f32[2,2048,128]{2,1,0:T(8,128)} %get-tuple-element.177) | copy-start | bytes 6291460 | tf_op jit(solution)/shard_map/while
  247.1 4.5 %copy-start.2 = (f32[2,2048,128]{2,1,0:T(8,128)}, f32[2,2048,128]{2,1,0:T(8,128)S(1)}, u32[]{:S(2)}) copy-start(f32[2,2048,128]{2,1,0:T(8,128)S(1)} %fusion.73) | copy-start | bytes 6291460 | tf_op jit(solution)/shard_map/while
  255.4 3.9 %copy-start.1 = (f32[2,2048,128]{2,1,0:T(8,128)S(1)}, f32[2,2048,128]{2,1,0:T(8,128)}, u32[]{:S(2)}) copy-start(f32[2,2048,128]{2,1,0:T(8,128)} %get-tuple-element.177) | copy-start | bytes 6291460 | tf_op jit(solution)/shard_map/while
  257.7 2.7 copy-start.6
  260.4 4.5 %copy-start.2 = (f32[2,2048,128]{2,1,0:T(8,128)}, f32[2,2048,128]{2,1,0:T(8,128)S(1)}, u32[]{:S(2)}) copy-start(f32[2,2048,128]{2,1,0:T(8,128)S(1)} %fusion.73) | copy-start | bytes 6291460 | tf_op jit(solution)/shard_map/while
  268.8 3.9 %copy-start.1 = (f32[2,2048,128]{2,1,0:T(8,128)S(1)}, f32[2,2048,128]{2,1,0:T(8,128)}, u32[]{:S(2)}) copy-start(f32[2,2048,128]{2,1,0:T(8,128)} %get-tuple-element.177) | copy-start | bytes 6291460 | tf_op jit(solution)/shard_map/while
  271.0 2.7 copy-start.6
  273.7 4.5 %copy-start.2 = (f32[2,2048,128]{2,1,0:T(8,128)}, f32[2,2048,128]{2,1,0:T(8,128)S(1)}, u32[]{:S(2)}) copy-start(f32[2,2048,128]{2,1,0:T(8,128)S(1)} %fusion.73) | copy-start | bytes 6291460 | tf_op jit(solution)/shard_map/while
  282.4 51.7 %reduce-scatter.4.cloned.1.call-start = ((), (), s32[]{:S(2)}) async-start(), calls=%async_computation.8 | async-start | bytes 1310720 | tf_op jit(solution)/shard_map/reduce_scatter | solution.py:101
  282.4 2.9 copy-start.3
  285.3 76.7 %reduce-scatter.6.cloned.1.call-start = ((), (), s32[]{:S(2)}) async-start(), calls=%async_computation.9 | async-start | bytes 1310720 | tf_op jit(solution)/shard_map/reduce_scatter | solution.py:104
  (14 other events, 28.8 us)
Sparse Core Ops, SparseCore 0:
  73.9 16.9 all-gather.11
  93.0 16.6 all-gather.9
  111.9 16.6 all-gather.7
  130.1 45.6 all-gather.13
  177.2 44.4 all-gather.15
  282.5 23.5 reduce-scatter.7
  309.2 24.8 reduce-scatter.3
  337.2 24.8 reduce-scatter.5
where the time goes:
time: 370 us; the launch traced here: 369 us
  waiting for transfers between devices  232 us (63%)
  local copies, waits for them, and re-layouts  36.9 us (10%)
  matrix products  30.5 us (8%)
  other arithmetic  29.7 us (8%)
  between operations  14.3 us (4%)
  blocking collectives  12.9 us (3%)
  loops' own time  8.17 us (2%)
  starting transfers between devices  4.77 us (1%)
    all_gather x1, waiting for transfers between devices, on_device(): lax.all_gather(tokens[0, 0], 'hidden', axis=1, tiled=True)  47.1 us
    all_gather x1, waiting for transfers between devices, on_device(): lax.all_gather(grad_out[0, 0], 'hidden', axis=1, tiled=True)  45.9 us
    reduce_scatter x1, waiting for transfers between devices, on_device(): lax.psum_scatter(totals[1].astype(jnp.bfloat16), 'dp', scatter_dimension=...  27.9 us
    reduce_scatter x1, waiting for transfers between devices, on_device(): lax.psum_scatter(totals[0].astype(jnp.bfloat16), 'dp', scatter_dimension=...  27.9 us
    reduce_scatter x1, waiting for transfers between devices, on_device(): lax.psum_scatter(totals[2].astype(jnp.bfloat16), 'dp', scatter_dimension=...  19.6 us
    all_gather x1, waiting for transfers between devices, on_device(): lax.all_gather(moved[2], 'dp', axis=2, tiled=True)  18.9 us
    all_gather x1, waiting for transfers between devices, on_device(): lax.all_gather(moved[1], 'dp', axis=1, tiled=True)  18.9 us
    dot_general x12, matrix products, contract_rows(): lax.dot_general(left, right, (((0,), (0,)), ((), ())), preferred_element_...  17.5 us
  transfers between devices with their start and end apart: 9, of which 9 were waited for; matrix products, arithmetic and copies ran while one was open for 2% of the time, Pallas kernels for 0%

commit v1 on v0

--- a/solution.py
+++ b/solution.py
@@ -4,6 +4,18 @@
 from jax.sharding import PartitionSpec as P
 
 BLOCK = 128
+
+
+def gather_by_bits(shard, axis, dim):
+    ways, here, hop = (lax.axis_size(axis), lax.axis_index(axis), shard.shape[dim])
+    line, have = (shard, 1)
+    while have < ways:
+        line = jnp.concatenate(
+            [line, lax.ppermute(line, axis, [(d, (d - have) % ways) for d in range(ways)])],
+            axis=dim,
+        )
+        have = 2 * have
+    return jnp.roll(line, here * hop, axis=dim)
 
 
 def contract_rows(left, right):
@@ -82,7 +94,7 @@
         lax.all_gather(moved[2], "dp", axis=2, tiled=True),
     )
     rows_full, grads_full = (
-        lax.all_gather(tokens[0, 0], "hidden", axis=1, tiled=True),
+        gather_by_bits(tokens[0, 0], "hidden", 1),
         lax.all_gather(grad_out[0, 0], "hidden", axis=1, tiled=True),
     )
     blocks = rows_full.shape[0] // BLOCK

time: 370 us -> 335 us (0.905)
  waiting for transfers between devices: 232 us -> 179 us
  matrix products: 30.5 us -> 51.4 us
  local copies, waits for them, and re-layouts: 36.9 us -> 27.4 us
  starting transfers between devices: 4.77 us -> 9.03 us
    ppermute x0 -> x2, waiting for transfers between devices: none -> 53 us  [gather_by_bits(): lax.ppermute(line, axis, [(d, (d - have) % ways) for d in range(ways)])]
    all_gather x1 -> x0, waiting for transfers between devices: 47.1 us -> none  [on_device(): lax.all_gather(tokens[0, 0], 'hidden', axis=1, tiled=True)]
    dot_general x12, matrix products: 17.5 us -> 38.9 us  [contract_rows(): lax.dot_general(left, right, (((0,), (0,)), ((), ())), preferred_element_...]
    all_gather x1, waiting for transfers between devices: 18.9 us -> 0.02 us  [on_device(): lax.all_gather(moved[2], 'dp', axis=2, tiled=True)]
    all_gather x1, waiting for transfers between devices: 18.9 us -> 0.02 us  [on_device(): lax.all_gather(moved[1], 'dp', axis=1, tiled=True)]
    all_gather x1, waiting for transfers between devices: 12.6 us -> 0.02 us  [on_device(): lax.all_gather(moved[0], 'dp', axis=1, tiled=True)]
    while x48 -> x0, local copies, waits for them, and re-layouts: 10 us -> none
    reduce_scatter x1, waiting for transfers between devices: 27.9 us -> 18.3 us  [on_device(): lax.psum_scatter(totals[0].astype(jnp.bfloat16), 'dp', scatter_dimension=...]
  transfers between devices with their start and end apart: 9 -> 10, of which waited for: 9 -> 7; matrix products, arithmetic and copies ran while one was open for 2% -> 3% of each run, Pallas kernels for 0% -> 0%
where the time goes in v1:
time: 335 us; the launch traced here: 333 us
  waiting for transfers between devices  179 us (53%)
  matrix products  51.4 us (15%)
  other arithmetic  31.3 us (9%)
  local copies, waits for them, and re-layouts  27.4 us (8%)
  between operations  14.4 us (4%)
  blocking collectives  12.9 us (4%)
  starting transfers between devices  9.03 us (3%)
  loops' own time  7.87 us (2%)
    ppermute x2, waiting for transfers between devices, gather_by_bits(): lax.ppermute(line, axis, [(d, (d - have) % ways) for d in range(ways)])  53 us
    all_gather x1, waiting for transfers between devices, on_device(): lax.all_gather(grad_out[0, 0], 'hidden', axis=1, tiled=True)  39.9 us
    dot_general x12, matrix products, contract_rows(): lax.dot_general(left, right, (((0,), (0,)), ((), ())), preferred_element_...  38.9 us
    reduce_scatter x1, waiting for transfers between devices, on_device(): lax.psum_scatter(totals[2].astype(jnp.bfloat16), 'dp', scatter_dimension=...  27.9 us
    reduce_scatter x1, waiting for transfers between devices, on_device(): lax.psum_scatter(totals[1].astype(jnp.bfloat16), 'dp', scatter_dimension=...  27.8 us
    reduce_scatter x1, waiting for transfers between devices, on_device(): lax.psum_scatter(totals[0].astype(jnp.bfloat16), 'dp', scatter_dimension=...  18.3 us
    all_to_all x1, blocking collectives, relocate(): lax.all_to_all(ordered, 'expert', split_axis=0, concat_axis=0, tiled=True)  12.9 us
    unnamed x24, local copies, waits for them, and re-layouts  12.7 us
  transfers between devices with their start and end apart: 10, of which 7 were waited for; matrix products, arithmetic and copies ran while one was open for 3% of the time, Pallas kernels for 0%

profile of v1, /device:TPU:0, one launch (start us, length us, event | category | flops | bytes accessed | tf_op | source)
XLA Modules:
  0.0 333.4 jit_solution(5477762657873851647)
XLA Ops:
  10.0 9.9 %maximum_bitcast_fusion = bf16[2,1,196608]{2,0,1:T(2,128)(2,1)S(1)} fusion(bf16[2,65536]{1,0:T(2,128)(2,1)S(1)} %bitcast.123, bf16[2,65536]{1,0:T(2,128)(2,1)S(1)} %get-tuple-element.92, bf16[2,65536]{1,0:T(2,128)(2,1)S(1)} %get-tuple-element.93), kind=kLoop, calls=%fused_computation.52 | loop fusion | flops 2359296 | bytes 1572864 | tf_op jit(solution)/shard_map/all_to_all | solution.py:77
  24.5 4.3 %all-to-all-start = ((bf16[2,2,98304]{2,1,0:T(2,128)(2,1)}), bf16[2,2,98304]{2,1,0:T(2,128)(2,1)S(1)}, u32[]{:S(2)}, u32[]{:S(2)}) async-start(bf16[2,2,98304]{2,1,0:T(2,128)(2,1)} %reshape.101), calls=%async_computation | async-start | bytes 1572864 | tf_op jit(solution)/shard_map/all_to_all | solution.py:77
  28.8 11.5 %all-to-all-done = bf16[2,2,98304]{2,1,0:T(2,128)(2,1)S(1)} async-done(((bf16[2,2,98304]{2,1,0:T(2,128)(2,1)}), bf16[2,2,98304]{2,1,0:T(2,128)(2,1)S(1)}, u32[]{:S(2)}, u32[]{:S(2)}) %all-to-all-start) | async-done | bytes 786464 | tf_op jit(solution)/shard_map/all_to_all | solution.py:77
  46.2 7.0 %broadcast_select_fusion = bf16[2,1,196608]{2,0,1:T(2,128)(2,1)S(1)} fusion(pred[2]{0:T(512)(128)(4,1)S(1)} %compare_and_fusion, bf16[2,98304]{1,0:T(2,128)(2,1)S(1)} %gather_fusion.1, bf16[2,98304]{1,0:T(2,128)(2,1)S(1)} %gather_fusion), kind=kLoop, calls=%fused_computation.50 | loop fusion | flops 1966080 | bytes 1572866 | tf_op jit(solution)/shard_map/jit(_take)/select_n | solution.py:78
  56.4 12.9 %all_to_all.21 = bf16[2,2,98304]{2,1,0:T(2,128)(2,1)S(1)} all-to-all(bf16[2,2,98304]{2,1,0:T(2,128)(2,1)S(1)} %reshape.103), channel_id=1, replica_groups=mesh['expert'=2,'hidden'=4,'dp'=4] {'expert'}, dimensions={0} | all-to-all | bytes 1572864 | tf_op jit(solution)/shard_map/all_to_all | solution.py:79
  76.1 3.8 %collective-permute-start = (bf16[512,512]{1,0:T(8,128)(2,1)S(1)}, bf16[512,512]{1,0:T(8,128)(2,1)S(1)}, u32[]{:S(2)}, u32[]{:S(2)}) collective-permute-start(bf16[512,512]{1,0:T(8,128)(2,1)S(1)} %bitcast.115), channel_id=1, source_target_pairs={{0,12},{4,0},{8,4},{12,8},{1,13},{5,1},{9,5},{13,9},{2,14},{6,2},{... | collective-permute-start | bytes 1572872 | tf_op jit(solution)/shard_map/ppermute | solution.py:14
  79.9 10.3 %collective-permute-done = bf16[512,512]{1,0:T(8,128)(2,1)S(1)} collective-permute-done((bf16[512,512]{1,0:T(8,128)(2,1)S(1)}, bf16[512,512]{1,0:T(8,128)(2,1)S(1)}, u32[]{:S(2)}, u32[]{:S(2)}) %collective-permute-start) | collective-permute-done | bytes 524320 | tf_op jit(solution)/shard_map/ppermute | solution.py:14
  92.6 42.7 %collective-permute-done.1 = bf16[512,1024]{1,0:T(8,128)(2,1)S(1)} collective-permute-done((bf16[512,1024]{1,0:T(8,128)(2,1)S(1)}, bf16[512,1024]{1,0:T(8,128)(2,1)S(1)}, u32[]{:S(2)}, u32[]{:S(2)}) %collective-permute-start.1) | collective-permute-done | bytes 1048608 | tf_op jit(solution)/shard_map/ppermute | solution.py:14
  135.8 39.9 %all-gather.12.cloned.1.call-done = bf16[1,1,512,2048]{3,2,1,0:T(8,128)(2,1)} async-done(((bf16[1,1,512,512]{3,2,1,0:T(8,128)(2,1)}), bf16[1,1,512,2048]{3,2,1,0:T(8,128)(2,1)}) %all-gather.12.cloned.1.call-update) | async-done | bytes 2097168 | tf_op jit(solution)/shard_map/all_gather | solution.py:98
  180.3 64.0 %while.14 = (s32[]{:T(128)}, f32[2,2048,128]{2,1,0:T(8,128)}, f32[2,2048,128]{2,1,0:T(8,128)}, f32[2,128,2048]{2,1,0:T(8,128)}, s32[4]{0:T(128)S(1)}, /*index=5*...) while((s32[]{:T(128)}, f32[2,2048,128]{2,1,0:T(8,128)}, ...), condition=%wide.region_3.4_spmd, body=%wide.region_2.3_spmd.sunk | while | flops 403849216 | bytes 11669723 | solution.py:68
  186.5 3.2 fusion.72
  189.7 3.2 fusion.73
  192.9 3.4 %fusion.74 = f32[2,128,2048]{2,1,0:T(8,128)} fusion(f32[2,128,2048]{2,1,0:T(8,128)} %get-tuple-element.178, s32[]{:T(128)S(6)} %select_n.55, bf16[4,128,2048]{2,1,0:T(8,128)(2,1)} %get-tuple-element.195, s32[]{:T(128)} %get-tuple-element.175, f32[128,128]{1,0:T(8,128)S(1)} %fusion.71, f32[]{:T(128)} %bitcast.112, f32[128,128]{1,0:T(8,128)S(1)} %fusion.69), kind=kOutput, calls=%fused_computation.10.clone.1 | convolution fusion | flops 67485696 | bytes 2753540 | tf_op jit(solution)/shard_map/while/body/eval_jaxpr/dot_general | solution.py:22
  202.5 3.2 fusion.72
  205.7 3.2 fusion.73
  208.9 3.4 %fusion.74 = f32[2,128,2048]{2,1,0:T(8,128)} fusion(f32[2,128,2048]{2,1,0:T(8,128)} %get-tuple-element.178, s32[]{:T(128)S(6)} %select_n.55, bf16[4,128,2048]{2,1,0:T(8,128)(2,1)} %get-tuple-element.195, s32[]{:T(128)} %get-tuple-element.175, f32[128,128]{1,0:T(8,128)S(1)} %fusion.71, f32[]{:T(128)} %bitcast.112, f32[128,128]{1,0:T(8,128)S(1)} %fusion.69), kind=kOutput, calls=%fused_computation.10.clone.1 | convolution fusion | flops 67485696 | bytes 2753540 | tf_op jit(solution)/shard_map/while/body/eval_jaxpr/dot_general | solution.py:22
  218.5 3.2 fusion.72
  224.9 3.4 %fusion.74 = f32[2,128,2048]{2,1,0:T(8,128)} fusion(f32[2,128,2048]{2,1,0:T(8,128)} %get-tuple-element.178, s32[]{:T(128)S(6)} %select_n.55, bf16[4,128,2048]{2,1,0:T(8,128)(2,1)} %get-tuple-element.195, s32[]{:T(128)} %get-tuple-element.175, f32[128,128]{1,0:T(8,128)S(1)} %fusion.71, f32[]{:T(128)} %bitcast.112, f32[128,128]{1,0:T(8,128)S(1)} %fusion.69), kind=kOutput, calls=%fused_computation.10.clone.1 | convolution fusion | flops 67485696 | bytes 2753540 | tf_op jit(solution)/shard_map/while/body/eval_jaxpr/dot_general | solution.py:22
  234.5 3.2 fusion.72
  237.7 3.2 fusion.73
  240.9 3.4 %fusion.74 = f32[2,128,2048]{2,1,0:T(8,128)} fusion(f32[2,128,2048]{2,1,0:T(8,128)} %get-tuple-element.178, s32[]{:T(128)S(6)} %select_n.55, bf16[4,128,2048]{2,1,0:T(8,128)(2,1)} %get-tuple-element.195, s32[]{:T(128)} %get-tuple-element.175, f32[128,128]{1,0:T(8,128)S(1)} %fusion.71, f32[]{:T(128)} %bitcast.112, f32[128,128]{1,0:T(8,128)S(1)} %fusion.69), kind=kOutput, calls=%fused_computation.10.clone.1 | convolution fusion | flops 67485696 | bytes 2753540 | tf_op jit(solution)/shard_map/while/body/eval_jaxpr/dot_general | solution.py:22
  252.6 18.3 %reduce-scatter.4.cloned.1.call-done = bf16[2,512,128]{2,1,0:T(8,128)(2,1)} async-done(((bf16[2,2048,128]{2,1,0:T(8,128)(2,1)}), bf16[2,512,128]{2,1,0:T(8,128)(2,1)}) %reduce-scatter.4.cloned.1.call-update) | async-done | bytes 262160 | tf_op jit(solution)/shard_map/reduce_scatter | solution.py:113
  270.8 27.8 %reduce-scatter.6.cloned.1.call-done = bf16[2,512,128]{2,1,0:T(8,128)(2,1)} async-done(((bf16[2,2048,128]{2,1,0:T(8,128)(2,1)}), bf16[2,512,128]{2,1,0:T(8,128)(2,1)}) %reduce-scatter.6.cloned.1.call-update) | async-done | bytes 262160 | tf_op jit(solution)/shard_map/reduce_scatter | solution.py:116
  298.6 27.9 %reduce-scatter.8.cloned.1.call-done = bf16[2,128,512]{2,1,0:T(8,128)(2,1)} async-done(((bf16[2,128,2048]{2,1,0:T(8,128)(2,1)}), bf16[2,128,512]{2,1,0:T(8,128)(2,1)}) %reduce-scatter.8.cloned.1.call-update) | async-done | bytes 262160 | tf_op jit(solution)/shard_map/reduce_scatter | solution.py:119
  (87 shorter events, 59.1 us)
Async XLA Ops:
  20.4 8.4 %copy-start.2 = (s32[2]{0:T(128)S(1)}, s32[2]{0:T(128)}, u32[]{:S(2)}) copy-start(s32[2]{0:T(128)} %param.14) | copy-start | bytes 28
  24.5 15.8 %all-to-all-start = ((bf16[2,2,98304]{2,1,0:T(2,128)(2,1)}), bf16[2,2,98304]{2,1,0:T(2,128)(2,1)S(1)}, u32[]{:S(2)}, u32[]{:S(2)}) async-start(bf16[2,2,98304]{2,1,0:T(2,128)(2,1)} %reshape.101), calls=%async_computation | async-start | bytes 1572864 | tf_op jit(solution)/shard_map/all_to_all | solution.py:77
  28.8 107.0 %all-gather.10.cloned.1.call-start = ((), (), s32[]{:S(2)}) async-start(), calls=%async_computation.7 | async-start | bytes 1310720 | tf_op jit(solution)/shard_map/all_gather | solution.py:92
  72.5 3.6 %copy-start.1 = (bf16[1,1,512,512]{3,2,1,0:T(8,128)(2,1)S(1)}, bf16[1,1,512,512]{3,2,1,0:T(8,128)(2,1)}, u32[]{:S(2)}) copy-start(bf16[1,1,512,512]{3,2,1,0:T(8,128)(2,1)} %param.9) | copy-start | bytes 1572868
  73.8 62.0 %all-gather.6.cloned.1.call-start = ((), (), s32[]{:S(2)}) async-start(), calls=%async_computation.5 | async-start | bytes 1310720 | tf_op jit(solution)/shard_map/all_gather | solution.py:94
  73.9 17.2 %copy-start.3 = (s32[1,1,2]{2,1,0:T(1,128)S(1)}, s32[1,1,2]{2,1,0:T(1,128)}, u32[]{:S(2)}) copy-start(s32[1,1,2]{2,1,0:T(1,128)} %param.15) | copy-start | bytes 28
  74.6 61.2 %all-gather.8.cloned.1.call-start = ((), (), s32[]{:S(2)}) async-start(), calls=%async_computation.6 | async-start | bytes 1310720 | tf_op jit(solution)/shard_map/all_gather | solution.py:93
  75.5 100.3 %all-gather.12.cloned.1.call-start = ((), (), s32[]{:S(2)}) async-start(), calls=%async_computation.11 | async-start | bytes 2621440 | tf_op jit(solution)/shard_map/all_gather | solution.py:98
  76.0 194.8 %reduce-scatter.4.cloned.1.call-start = ((), (), s32[]{:S(2)}) async-start(), calls=%async_computation.8 | async-start | bytes 1310720 | tf_op jit(solution)/shard_map/reduce_scatter | solution.py:113
  76.1 14.1 %collective-permute-start = (bf16[512,512]{1,0:T(8,128)(2,1)S(1)}, bf16[512,512]{1,0:T(8,128)(2,1)S(1)}, u32[]{:S(2)}, u32[]{:S(2)}) collective-permute-start(bf16[512,512]{1,0:T(8,128)(2,1)S(1)} %bitcast.115), channel_id=1, source_target_pairs={{0,12},{4,0},{8,4},{12,8},{1,13},{5,1},{9,5},{13,9},{2,14},{6,2},{... | collective-permute-start | bytes 1572872 | tf_op jit(solution)/shard_map/ppermute | solution.py:14
  90.4 44.9 %collective-permute-start.1 = (bf16[512,1024]{1,0:T(8,128)(2,1)S(1)}, bf16[512,1024]{1,0:T(8,128)(2,1)S(1)}, u32[]{:S(2)}, u32[]{:S(2)}) collective-permute-start(bf16[512,1024]{1,0:T(8,128)(2,1)S(1)} %pad_maximum_fusion), channel_id=1, source_target_pairs={{0,8},{4,12},{8,0},{12,4},{1,9},{5,13},{9,1},{13,5},{2,10},{6,14},... | collective-permute-start | bytes 3145736 | tf_op jit(solution)/shard_map/ppermute | solution.py:14
  177.2 3.0 copy-start
  247.0 51.7 %reduce-scatter.6.cloned.1.call-start = ((), (), s32[]{:S(2)}) async-start(), calls=%async_computation.9 | async-start | bytes 1310720 | tf_op jit(solution)/shard_map/reduce_scatter | solution.py:116
  249.8 76.8 %reduce-scatter.8.cloned.1.call-start = ((), (), s32[]{:S(2)}) async-start(), calls=%async_computation.10 | async-start | bytes 1310720 | tf_op jit(solution)/shard_map/reduce_scatter | solution.py:119
Sparse Core Ops, SparseCore 0:
  73.9 16.9 all-gather.9
  93.1 16.6 all-gather.5
  111.9 16.6 all-gather.7
  130.1 45.6 all-gather.11
  247.1 23.7 reduce-scatter.3
  273.8 24.7 reduce-scatter.5
  301.7 24.7 reduce-scatter.7
